TPU v7x, 32 devices: a whole 2x2x4 slice. The times are simulated.
32 devices in a mesh: section: 2 (over y), dp: 4 (over x, core), expert: 4 (over z).
Axes of the slice: x: 2, y: 2, z: 4, core: 2. Of those that a mesh axis runs over, the one named last changes fastest.
Arguments:
- upstream: bfloat16 [2, 256, 4096], P('section', 'expert', 'dp'), may hold values from -6 to 6
- routes: int32 [2, 256, 2], P('section', 'expert'), may hold values from 0 to 3, all different within a row; in each aligned block of 64 rows (0 to 63, 64 to 127, ..., all dimensions but the last counted through in order) at most 48 rows name the same one
- gate_weights: bfloat16 [2, 256, 2], P('section', 'expert'), may hold values from 0.049804688 to 0.5
- w_gate: bfloat16 [2, 4, 4096, 768], P('section', 'expert', 'dp'), may hold values from -0.09375 to 0.09375
- w_up: bfloat16 [2, 4, 4096, 768], P('section', 'expert', 'dp'), may hold values from -0.09375 to 0.09375
- w_down: bfloat16 [2, 4, 768, 4096], P('section', 'expert', None, 'dp'), may hold values from -0.21875 to 0.21875
- saved_gate: bfloat16 [2, 4, 4, 48, 768], P('section', 'expert'), may hold values from -6 to 6
- saved_up: bfloat16 [2, 4, 4, 48, 768], P('section', 'expert'), may hold values from -6 to 6
Outputs:
- handed: bfloat16 [2, 256, 4096], P('section', 'expert', 'dp')
- gate_grads: bfloat16 [2, 256, 2], P('section', 'expert')
Inputs may be any that keep to these rules, and one draw needn't show every extreme that they name: `routes`: each token names 2 different experts; among the 64 tokens of one device no expert is named by more than 48 tokens, and in every draw some expert is named by exactly 48 tokens of some device.
All inputs are finite; a program needn't handle non-finite values.
Results may differ from a plain program's by a relative error of at most 0.015.
Values may be sent and summed in bfloat16 or wider, within the bound.
No kernel may reach another device: no remote copies, remote signals or barrier semaphores. Data moves between devices by JAX's collectives and lax.ppermute only.
A program may use at most 64 MiB of HBM per device.

v0:
```python
import jax
import jax.numpy as jnp
from jax import lax
from jax.sharding import PartitionSpec as P


def shifted(value, axis, steps):
    count = lax.axis_size(axis)
    initial, last = (max(0, -steps), min(count, count - steps))
    return lax.ppermute(value, axis, [(source, source + steps) for source in range(initial, last)])


def slot_tables(route_block, experts, capacity):
    tokens_here, picks_here = route_block.shape
    labels = jnp.arange(experts, dtype=jnp.int32)
    onehot = (route_block[:, :, None] == labels[None, None, :]).astype(jnp.int32)
    per_token = jnp.sum(onehot, axis=1)
    earlier = jnp.cumsum(per_token, axis=0) - per_token
    slot = jnp.sum(onehot * earlier[:, None, :], axis=2)
    target = (route_block * capacity + slot).reshape(-1)
    places = jnp.arange(experts * capacity, dtype=jnp.int32)
    placement = (places[:, None] == target[None, :]).astype(jnp.bfloat16)
    by_token = jnp.sum(placement.reshape(experts * capacity, tokens_here, picks_here), axis=2)
    return (placement, by_token)


def swiglu_back(hidden_grad, gate_pre, up_pre):
    gate_val = gate_pre.astype(jnp.float32)
    up_val = up_pre.astype(jnp.float32)
    sigmoid_val = jax.nn.sigmoid(gate_val)
    silu_val = gate_val * sigmoid_val
    gate_back = (
        hidden_grad * up_val * sigmoid_val * (1.0 + gate_val * (1.0 - sigmoid_val))
    ).astype(jnp.bfloat16)
    up_back = (hidden_grad * silu_val).astype(jnp.bfloat16)
    return (gate_back, up_back)


def per_device(upstream, routes, gate_weights, w_gate, w_up, w_down, saved_gate, saved_up):
    grads_here = upstream[0]
    route_block = routes[0]
    experts = lax.axis_size("expert")
    groups = saved_gate.shape[2]
    capacity = saved_gate.shape[3]
    slot_count = groups * capacity
    feature_width = grads_here.shape[1]
    placement, by_token = slot_tables(route_block, experts, capacity)
    send_rows = jnp.dot(by_token, grads_here, preferred_element_type=jnp.float32).astype(
        jnp.bfloat16
    )
    send_gate = jnp.dot(
        placement, gate_weights[0].reshape(-1), preferred_element_type=jnp.float32
    ).astype(jnp.bfloat16)
    recv_rows, recv_gate = (
        lax.all_to_all(
            send_rows.reshape(experts, capacity, feature_width),
            "expert",
            split_axis=0,
            concat_axis=0,
            tiled=True,
        ),
        lax.all_to_all(
            send_gate.reshape(experts, capacity), "expert", split_axis=0, concat_axis=0, tiled=True
        ),
    )
    slot_rows = recv_rows.reshape(slot_count, feature_width)
    slot_gate = recv_gate.reshape(slot_count)
    gate_pre = saved_gate[0, 0].reshape(slot_count, -1)
    up_pre = saved_up[0, 0].reshape(slot_count, -1)
    down_local = w_down[0, 0]
    scaled = (slot_gate.astype(jnp.float32)[:, None] * slot_rows.astype(jnp.float32)).astype(
        jnp.bfloat16
    )
    hidden_part = lax.dot_general(
        scaled, down_local, (((1,), (1,)), ((), ())), preferred_element_type=jnp.float32
    )
    gate_val = gate_pre.astype(jnp.float32)
    hidden = (gate_val * jax.nn.sigmoid(gate_val) * up_pre.astype(jnp.float32)).astype(jnp.bfloat16)
    expert_out = jnp.dot(hidden, down_local, preferred_element_type=jnp.float32).astype(
        jnp.bfloat16
    )
    hidden_grad = lax.psum(hidden_part.astype(jnp.bfloat16), "dp").astype(jnp.float32)
    gate_back, up_back = swiglu_back(hidden_grad, gate_pre, up_pre)
    extra_back = expert_out.reshape(groups, capacity, feature_width)
    contract = (((1,), (1,)), ((), ()))
    row_grad = (
        lax.dot_general(gate_back, w_gate[0, 0], contract, preferred_element_type=jnp.float32)
        + lax.dot_general(up_back, w_up[0, 0], contract, preferred_element_type=jnp.float32)
    ).astype(jnp.bfloat16)
    back_rows, back_extra = (
        lax.all_to_all(
            row_grad.reshape(groups, capacity, feature_width),
            "expert",
            split_axis=0,
            concat_axis=0,
            tiled=True,
        ),
        lax.all_to_all(extra_back, "expert", split_axis=0, concat_axis=0, tiled=True),
    )
    inner_back = jnp.sum(
        back_extra.reshape(slot_count, feature_width).astype(jnp.float32)
        * send_rows.astype(jnp.float32),
        axis=1,
    )
    slot_back = lax.psum(inner_back.astype(jnp.bfloat16), "dp")
    routed_sum = lax.dot_general(
        by_token,
        back_rows.reshape(slot_count, feature_width),
        (((0,), (0,)), ((), ())),
        preferred_element_type=jnp.float32,
    )
    layer_grad = (grads_here.astype(jnp.float32) + routed_sum).astype(jnp.bfloat16)
    handed = shifted(layer_grad, "section", -1)
    gate_grads = (
        jnp.dot(slot_back, placement, preferred_element_type=jnp.float32)
        .astype(jnp.bfloat16)
        .reshape(route_block.shape)
    )
    return (handed[None], gate_grads[None])


def solution(mesh):
    placed = (
        P("section", "expert", "dp"),
        P("section", "expert", None),
        P("section", "expert", None),
        P("section", "expert", "dp", None),
        P("section", "expert", "dp", None),
        P("section", "expert", None, "dp"),
        P("section", "expert", None, None, None),
        P("section", "expert", None, None, None),
    )
    return jax.shard_map(
        per_device,
        mesh=mesh,
        in_specs=placed,
        out_specs=(P("section", "expert", "dp"), P("section", "expert", None)),
        check_vma=False,
    )
```

profile of v0, /device:TPU:0, one launch (start us, length us, event | category | flops | bytes accessed | tf_op | source)
XLA Modules:
  0.0 117.4 jit_solution(11747973921744513255)
XLA Ops:
  7.2 1.4 %fusion.35 = bf16[1,1,4,48,768]{4,3,2,1,0:T(8,128)(2,1)S(1)} fusion(bf16[1,1,4,48,768]{4,3,2,1,0:T(8,128)(2,1)} %param.14, bf16[1,1,4,48,768]{4,3,2,1,0:T(8,128)(2,1)} %param.15), kind=kLoop, calls=%fused_computation.39 | loop fusion | flops 1179648 | bytes 884736 | tf_op jit(solution)/shard_map/convert_element_type | solution.py:78
  8.6 0.2 copy-done
  8.8 1.2 %fusion.14 = bf16[192,1024]{1,0:T(8,128)(2,1)} fusion(bf16[192,768]{1,0:T(8,128)(2,1)S(1)} %bitcast.76, bf16[1,1,768,1024]{3,2,1,0:T(8,128)(2,1)S(1)} %copy-done), kind=kOutput, calls=%fused_computation.10 | convolution fusion | flops 302186496 | bytes 2260992 | tf_op jit(solution)/shard_map/dot_general | solution.py:79
  10.0 6.3 %all-to-all-start.3 = ((bf16[4,48,1024]{2,1,0:T(8,128)(2,1)}), bf16[4,48,1024]{2,1,0:T(8,128)(2,1)S(1)}, u32[]{:S(2)}, u32[]{:S(2)}) async-start(bf16[4,48,1024]{2,1,0:T(8,128)(2,1)} %bitcast.15), calls=%async_computation.3 | async-start | bytes 786432 | tf_op jit(solution)/shard_map/all_to_all | solution.py:98
  17.6 0.7 all_to_all.20
  18.4 9.7 %all-to-all-done.3 = bf16[4,48,1024]{2,1,0:T(8,128)(2,1)S(1)} async-done(((bf16[4,48,1024]{2,1,0:T(8,128)(2,1)}), bf16[4,48,1024]{2,1,0:T(8,128)(2,1)S(1)}, u32[]{:S(2)}, u32[]{:S(2)}) %all-to-all-start.3) | async-done | bytes 393248 | tf_op jit(solution)/shard_map/all_to_all | solution.py:98
  28.0 3.2 %all-to-all-start = ((bf16[4,1,48]{2,1,0:T(2,128)(2,1)}), bf16[4,1,48]{2,1,0:T(2,128)(2,1)S(1)}, u32[]{:S(2)}, u32[]{:S(2)}) async-start(bf16[4,1,48]{2,1,0:T(2,128)(2,1)} %all_to_all.20), calls=%async_computation | async-start | bytes 4096 | tf_op jit(solution)/shard_map/all_to_all | solution.py:62
  31.3 1.0 fusion.22
  32.3 4.4 %all-to-all-done = bf16[4,1,48]{2,1,0:T(2,128)(2,1)S(1)} async-done(((bf16[4,1,48]{2,1,0:T(2,128)(2,1)}), bf16[4,1,48]{2,1,0:T(2,128)(2,1)S(1)}, u32[]{:S(2)}, u32[]{:S(2)}) %all-to-all-start) | async-done | bytes 416 | tf_op jit(solution)/shard_map/all_to_all | solution.py:62
  36.7 3.5 %all-to-all-start.1 = ((bf16[4,48,1024]{2,1,0:T(8,128)(2,1)}), bf16[4,48,1024]{2,1,0:T(8,128)(2,1)S(1)}, u32[]{:S(2)}, u32[]{:S(2)}) async-start(bf16[4,48,1024]{2,1,0:T(8,128)(2,1)} %bitcast.4), calls=%async_computation.1 | async-start | bytes 786432 | tf_op jit(solution)/shard_map/all_to_all | solution.py:55
  40.2 10.0 %all-to-all-done.1 = bf16[4,48,1024]{2,1,0:T(8,128)(2,1)S(1)} async-done(((bf16[4,48,1024]{2,1,0:T(8,128)(2,1)}), bf16[4,48,1024]{2,1,0:T(8,128)(2,1)S(1)}, u32[]{:S(2)}, u32[]{:S(2)}) %all-to-all-start.1) | async-done | bytes 393248 | tf_op jit(solution)/shard_map/all_to_all | solution.py:55
  50.4 1.4 %fusion.17 = bf16[192,768]{1,0:T(8,128)(2,1)} fusion(bf16[192,1024]{1,0:T(8,128)(2,1)S(1)} %bitcast.75, bf16[1,1,768,1024]{3,2,1,0:T(8,128)(2,1)S(1)} %copy-done), kind=kOutput, calls=%fused_computation.12 | convolution fusion | flops 302137344 | bytes 2260992 | tf_op jit(solution)/shard_map/dot_general | solution.py:74
  51.8 31.7 %all-reduce.2.cloned.1.call-done = bf16[192,768]{1,0:T(8,128)(2,1)} async-done(((bf16[192,768]{1,0:T(8,128)(2,1)}), bf16[192,768]{1,0:T(8,128)(2,1)}) %all-reduce.2.cloned.1.call-update) | async-done | bytes 294928 | tf_op jit(solution)/shard_map/psum | solution.py:82
  83.5 1.4 %fusion.25 = (bf16[192,768]{1,0:T(8,128)(2,1)S(1)}, bf16[192,768]{1,0:T(8,128)(2,1)S(1)}) fusion(bf16[192,768]{1,0:T(8,128)(2,1)} %all-reduce.2.cloned.1.call-done, bf16[1,1,4,48,768]{4,3,2,1,0:T(8,128)(2,1)S(1)} %copy-done.3, bf16[1,1,4,48,768]{4,3,2,1,0:T(8,128)(2,1)} %param.15), kind=kLoop, calls=%fused_computation.24 | loop fusion | flops 2359296 | bytes 1474560 | tf_op jit(solution)/shard_map/convert_element_type | solution.py:34
  84.9 0.7 fusion
  85.5 0.7 copy-done.1
  86.3 1.4 %fusion.11 = bf16[192,1024]{1,0:T(8,128)(2,1)} fusion(f32[192,1024]{1,0:T(8,128)S(1)} %fusion, bf16[192,768]{1,0:T(8,128)(2,1)S(1)} %get-tuple-element.12, bf16[1,1,1024,768]{3,2,1,0:T(8,128)(2,1)S(1)} %copy-done.1), kind=kOutput, calls=%fused_computation.9 | convolution fusion | flops 302383104 | bytes 3047424 | tf_op jit(solution)/shard_map/dot_general | solution.py:87
  87.7 4.6 %all-to-all-start.2 = ((bf16[4,48,1024]{2,1,0:T(8,128)(2,1)}), bf16[4,48,1024]{2,1,0:T(8,128)(2,1)S(1)}, u32[]{:S(2)}, u32[]{:S(2)}) async-start(bf16[4,48,1024]{2,1,0:T(8,128)(2,1)} %bitcast.11), calls=%async_computation.2 | async-start | bytes 786432 | tf_op jit(solution)/shard_map/all_to_all | solution.py:91
  92.3 5.9 %psum.15 = bf16[192]{0:T(256)(128)(2,1)S(1)} all-reduce(bf16[192]{0:T(256)(128)(2,1)S(1)} %get-tuple-element.14), channel_id=1, replica_groups=mesh['section'=2,'dp'=4,'expert'=4] {'dp'}, use_global_device_ids=true, to_apply=%region_6.7 | all-reduce | flops 192 | bytes 768 | tf_op jit(solution)/shard_map/psum | solution.py:105
  98.2 4.7 %all-to-all-done.2 = bf16[4,48,1024]{2,1,0:T(8,128)(2,1)S(1)} async-done(((bf16[4,48,1024]{2,1,0:T(8,128)(2,1)}), bf16[4,48,1024]{2,1,0:T(8,128)(2,1)S(1)}, u32[]{:S(2)}, u32[]{:S(2)}) %all-to-all-start.2) | async-done | bytes 393248 | tf_op jit(solution)/shard_map/all_to_all | solution.py:91
  103.1 1.3 %collective-permute-start = (bf16[64,1024]{1,0:T(8,128)(2,1)S(1)}, bf16[64,1024]{1,0:T(8,128)(2,1)S(1)}, u32[]{:S(2)}, u32[]{:S(2)}) collective-permute-start(bf16[64,1024]{1,0:T(8,128)(2,1)S(1)} %fusion.20), channel_id=1, source_target_pairs={{16,0},{17,1},{18,2},{19,3},{20,4},{21,5},{22,6},{23,7},{24,8},{25... | collective-permute-start | bytes 393224 | tf_op jit(solution)/shard_map/ppermute | solution.py:10
  104.7 0.6 copy.42
  105.3 4.6 %collective-permute-done = bf16[64,1024]{1,0:T(8,128)(2,1)S(1)} collective-permute-done((bf16[64,1024]{1,0:T(8,128)(2,1)S(1)}, bf16[64,1024]{1,0:T(8,128)(2,1)S(1)}, u32[]{:S(2)}, u32[]{:S(2)}) %collective-permute-start) | collective-permute-done | bytes 131104 | tf_op jit(solution)/shard_map/ppermute | solution.py:10
  109.9 0.7 copy.45
  (40 shorter events, 2.0 us)
Async XLA Ops:
  7.2 1.6 %copy-start = (bf16[1,1,768,1024]{3,2,1,0:T(8,128)(2,1)S(1)}, bf16[1,1,768,1024]{3,2,1,0:T(8,128)(2,1)}, u32[]{:S(2)}) copy-start(bf16[1,1,768,1024]{3,2,1,0:T(8,128)(2,1)} %param.13) | copy-start | bytes 4718596
  8.5 7.8 %copy-start.6 = (s32[1,64,2]{1,2,0:T(2,128)S(1)}, s32[1,64,2]{1,2,0:T(2,128)}, u32[]{:S(2)}) copy-start(s32[1,64,2]{1,2,0:T(2,128)} %param.9) | copy-start | bytes 1540
  8.8 7.9 %copy-start.7 = (bf16[1,64,2]{1,2,0:T(2,128)(2,1)S(1)}, bf16[1,64,2]{1,2,0:T(2,128)(2,1)}, u32[]{:S(2)}) copy-start(bf16[1,64,2]{1,2,0:T(2,128)(2,1)} %param.10) | copy-start | bytes 772
  8.8 22.5 %copy-start.4 = (bf16[1,64,1024]{2,1,0:T(8,128)(2,1)S(1)}, bf16[1,64,1024]{2,1,0:T(8,128)(2,1)}, u32[]{:S(2)}) copy-start(bf16[1,64,1024]{2,1,0:T(8,128)(2,1)} %param.8) | copy-start | bytes 393220
  10.0 18.0 %all-to-all-start.3 = ((bf16[4,48,1024]{2,1,0:T(8,128)(2,1)}), bf16[4,48,1024]{2,1,0:T(8,128)(2,1)S(1)}, u32[]{:S(2)}, u32[]{:S(2)}) async-start(bf16[4,48,1024]{2,1,0:T(8,128)(2,1)} %bitcast.15), calls=%async_computation.3 | async-start | bytes 786432 | tf_op jit(solution)/shard_map/all_to_all | solution.py:98
  28.0 8.7 %all-to-all-start = ((bf16[4,1,48]{2,1,0:T(2,128)(2,1)}), bf16[4,1,48]{2,1,0:T(2,128)(2,1)S(1)}, u32[]{:S(2)}, u32[]{:S(2)}) async-start(bf16[4,1,48]{2,1,0:T(2,128)(2,1)} %all_to_all.20), calls=%async_computation | async-start | bytes 4096 | tf_op jit(solution)/shard_map/all_to_all | solution.py:62
  36.7 13.5 %all-to-all-start.1 = ((bf16[4,48,1024]{2,1,0:T(8,128)(2,1)}), bf16[4,48,1024]{2,1,0:T(8,128)(2,1)S(1)}, u32[]{:S(2)}, u32[]{:S(2)}) async-start(bf16[4,48,1024]{2,1,0:T(8,128)(2,1)} %bitcast.4), calls=%async_computation.1 | async-start | bytes 786432 | tf_op jit(solution)/shard_map/all_to_all | solution.py:55
  40.2 43.3 %all-reduce.2.cloned.1.call-start = ((), (), s32[]{:S(2)}) async-start(), calls=%async_computation.4 | async-start | bytes 589824 | tf_op jit(solution)/shard_map/psum | solution.py:82
  50.2 33.2 %copy-start.3 = (bf16[1,1,4,48,768]{4,3,2,1,0:T(8,128)(2,1)S(1)}, bf16[1,1,4,48,768]{4,3,2,1,0:T(8,128)(2,1)}, u32[]{:S(2)}) copy-start(bf16[1,1,4,48,768]{4,3,2,1,0:T(8,128)(2,1)} %param.14) | copy-start | bytes 884740
  50.4 34.5 %copy-start.2 = (bf16[1,1,1024,768]{3,2,1,0:T(8,128)(2,1)S(1)}, bf16[1,1,1024,768]{3,2,1,0:T(8,128)(2,1)}, u32[]{:S(2)}) copy-start(bf16[1,1,1024,768]{3,2,1,0:T(8,128)(2,1)} %param.12) | copy-start | bytes 4718596
  84.9 1.4 %copy-start.1 = (bf16[1,1,1024,768]{3,2,1,0:T(8,128)(2,1)S(1)}, bf16[1,1,1024,768]{3,2,1,0:T(8,128)(2,1)}, u32[]{:S(2)}) copy-start(bf16[1,1,1024,768]{3,2,1,0:T(8,128)(2,1)} %param.11) | copy-start | bytes 4718596
  86.3 16.6 %copy-start.5 = (bf16[1,64,1024]{2,1,0:T(8,128)(2,1)S(1)}, bf16[1,64,1024]{2,1,0:T(8,128)(2,1)}, u32[]{:S(2)}) copy-start(bf16[1,64,1024]{2,1,0:T(8,128)(2,1)} %param.8) | copy-start | bytes 393220
  87.7 15.2 %all-to-all-start.2 = ((bf16[4,48,1024]{2,1,0:T(8,128)(2,1)}), bf16[4,48,1024]{2,1,0:T(8,128)(2,1)S(1)}, u32[]{:S(2)}, u32[]{:S(2)}) async-start(bf16[4,48,1024]{2,1,0:T(8,128)(2,1)} %bitcast.11), calls=%async_computation.2 | async-start | bytes 786432 | tf_op jit(solution)/shard_map/all_to_all | solution.py:91
  103.1 6.9 %collective-permute-start = (bf16[64,1024]{1,0:T(8,128)(2,1)S(1)}, bf16[64,1024]{1,0:T(8,128)(2,1)S(1)}, u32[]{:S(2)}, u32[]{:S(2)}) collective-permute-start(bf16[64,1024]{1,0:T(8,128)(2,1)S(1)} %fusion.20), channel_id=1, source_target_pairs={{16,0},{17,1},{18,2},{19,3},{20,4},{21,5},{22,6},{23,7},{24,8},{25... | collective-permute-start | bytes 393224 | tf_op jit(solution)/shard_map/ppermute | solution.py:10
Sparse Core Ops, SparseCore 0:
  51.9 31.5 all-reduce.1
where the time goes:
time: 118 us; the launch traced here: 117 us
  waiting for transfers between devices  65.1 us (55%)
  starting transfers between devices  19 us (16%)
  between operations  14.2 us (12%)
  matrix products  6.17 us (5%)
  blocking collectives  5.93 us (5%)
  local copies, waits for them, and re-layouts  4 us (3%)
  other arithmetic  3.1 us (3%)
    psum x1, waiting for transfers between devices, per_device(): lax.psum(hidden_part.astype(jnp.bfloat16), 'dp').astype(jnp.float32)  31.7 us
    all_to_all x1, waiting for transfers between devices, per_device(): lax.all_to_all(send_rows.reshape(experts, capacity, feature_width), 'expe...  10 us
    all_to_all x1, waiting for transfers between devices, per_device(): lax.all_to_all(extra_back, 'expert', split_axis=0, concat_axis=0, tiled=T...  9.65 us
    all_to_all x1, starting transfers between devices, per_device(): lax.all_to_all(extra_back, 'expert', split_axis=0, concat_axis=0, tiled=T...  6.35 us
    psum x1, blocking collectives, per_device(): slot_back = lax.psum(inner_back.astype(jnp.bfloat16), 'dp')  5.93 us
    all_to_all x1, waiting for transfers between devices, per_device(): lax.all_to_all(row_grad.reshape(groups, capacity, feature_width), 'expert...  4.65 us
    ppermute x1, waiting for transfers between devices, shifted(): lax.ppermute(value, axis, [(source, source + steps) for source in range(i...  4.65 us
    all_to_all x1, starting transfers between devices, per_device(): lax.all_to_all(row_grad.reshape(groups, capacity, feature_width), 'expert...  4.6 us
  transfers between devices with their start and end apart: 6, of which 6 were waited for; matrix products, arithmetic and copies ran while one was open for 3% of the time, Pallas kernels for 0%

commit v1 on v0

--- a/solution.py
+++ b/solution.py
@@ -2,6 +2,12 @@
 import jax.numpy as jnp
 from jax import lax
 from jax.sharding import PartitionSpec as P
+
+
+def gather_and_add(x, name):
+    pieces = lax.all_gather(x, name, axis=0, tiled=False)
+    total = pieces.sum(axis=0)
+    return total
 
 
 def shifted(value, axis, steps):
@@ -79,7 +85,7 @@
     expert_out = jnp.dot(hidden, down_local, preferred_element_type=jnp.float32).astype(
         jnp.bfloat16
     )
-    hidden_grad = lax.psum(hidden_part.astype(jnp.bfloat16), "dp").astype(jnp.float32)
+    hidden_grad = gather_and_add(hidden_part.astype(jnp.bfloat16), "dp").astype(jnp.float32)
     gate_back, up_back = swiglu_back(hidden_grad, gate_pre, up_pre)
     extra_back = expert_out.reshape(groups, capacity, feature_width)
     contract = (((1,), (1,)), ((), ()))

time: 118 us -> 107 us (0.907)
  waiting for transfers between devices: 65.1 us -> 46.5 us
  other arithmetic: 3.1 us -> 7.12 us
  matrix products: 6.17 us -> 8.65 us
    psum x1 -> x0, waiting for transfers between devices: 31.7 us -> none  [per_device(): lax.psum(hidden_part.astype(jnp.bfloat16), 'dp').astype(jnp.float32)]
    all_gather x0 -> x1, waiting for transfers between devices: none -> 16.7 us  [gather_and_add(): pieces = lax.all_gather(x, name, axis=0, tiled=False)]
    all_to_all x1, starting transfers between devices: 3.22 us -> 6.35 us  [per_device(): lax.all_to_all(send_gate.reshape(experts, capacity), 'expert', split_axis...]
    reduce_sum x0 -> x2, other arithmetic: none -> 2.7 us  [the longest x1 1.52 us: gather_and_add(): total = pieces.sum(axis=0)]
    all_to_all x1, waiting for transfers between devices: 4.43 us -> 2.23 us  [per_device(): lax.all_to_all(send_gate.reshape(experts, capacity), 'expert', split_axis...]
    all_to_all x1, starting transfers between devices: 6.35 us -> 4.73 us  [per_device(): lax.all_to_all(extra_back, 'expert', split_axis=0, concat_axis=0, tiled=T...]
    dot_general x1, matrix products: 0.66 us -> 2.21 us  [per_device(): lax.dot_general(up_back, w_up[0, 0], contract, preferred_element_type=jnp...]
    convert_element_type x1 -> x0, other arithmetic: 1.37 us -> none  [swiglu_back(): gate_back = (hidden_grad * up_val * sigmoid_val * (1.0 + gate_val * (1.0...]
  transfers between devices with their start and end apart: 6 -> 6, of which waited for: 6 -> 6; matrix products, arithmetic and copies ran while one was open for 3% -> 8% of each run, Pallas kernels for 0% -> 0%
where the time goes in v1:
time: 107 us; the launch traced here: 106 us
  waiting for transfers between devices  46.5 us (43%)
  starting transfers between devices  19.3 us (18%)
  between operations  14.2 us (13%)
  matrix products  8.65 us (8%)
  other arithmetic  7.12 us (7%)
  blocking collectives  5.98 us (6%)
  local copies, waits for them, and re-layouts  4.32 us (4%)
    all_gather x1, waiting for transfers between devices, gather_and_add(): pieces = lax.all_gather(x, name, axis=0, tiled=False)  16.7 us
    all_to_all x1, waiting for transfers between devices, per_device(): lax.all_to_all(send_rows.reshape(experts, capacity, feature_width), 'expe...  10.5 us
    all_to_all x1, waiting for transfers between devices, per_device(): lax.all_to_all(extra_back, 'expert', split_axis=0, concat_axis=0, tiled=T...  8.41 us
    all_to_all x1, starting transfers between devices, per_device(): lax.all_to_all(send_gate.reshape(experts, capacity), 'expert', split_axis...  6.35 us
    psum x1, blocking collectives, per_device(): slot_back = lax.psum(inner_back.astype(jnp.bfloat16), 'dp')  5.98 us
    all_to_all x1, starting transfers between devices, per_device(): lax.all_to_all(extra_back, 'expert', split_axis=0, concat_axis=0, tiled=T...  4.73 us
    ppermute x1, waiting for transfers between devices, shifted(): lax.ppermute(value, axis, [(source, source + steps) for source in range(i...  4.65 us
    all_to_all x1, waiting for transfers between devices, per_device(): lax.all_to_all(row_grad.reshape(groups, capacity, feature_width), 'expert...  4.04 us
  transfers between devices with their start and end apart: 6, of which 6 were waited for; matrix products, arithmetic and copies ran while one was open for 8% of the time, Pallas kernels for 0%

profile of v1, /device:TPU:0, one launch (start us, length us, event | category | flops | bytes accessed | tf_op | source)
XLA Modules:
  0.0 106.1 jit_solution(10828815765891260589)
XLA Ops:
  7.2 0.8 broadcast_multiply_fusion
  8.7 0.8 copy.40
  10.1 0.7 select_reduce_fusion
  11.2 0.7 all_to_all.20
  11.9 6.3 %all-to-all-start = ((bf16[4,1,48]{2,1,0:T(2,128)(2,1)}), bf16[4,1,48]{2,1,0:T(2,128)(2,1)S(1)}, u32[]{:S(2)}, u32[]{:S(2)}) async-start(bf16[4,1,48]{2,1,0:T(2,128)(2,1)} %all_to_all.20), calls=%async_computation | async-start | bytes 4096 | tf_op jit(solution)/shard_map/all_to_all | solution.py:68
  19.7 1.9 %convolution_convert_fusion = bf16[192,1024]{1,0:T(8,128)(2,1)} fusion(bf16[192,64]{0,1:T(8,128)(2,1)S(1)} %fusion.35, bf16[1,64,1024]{2,1,0:T(8,128)(2,1)} %param.8), kind=kOutput, calls=%fused_computation.11 | convolution fusion | flops 25362432 | bytes 548864 | tf_op jit(solution)/shard_map/dot_general | solution.py:54
  21.6 2.2 %all-to-all-done = bf16[4,1,48]{2,1,0:T(2,128)(2,1)S(1)} async-done(((bf16[4,1,48]{2,1,0:T(2,128)(2,1)}), bf16[4,1,48]{2,1,0:T(2,128)(2,1)S(1)}, u32[]{:S(2)}, u32[]{:S(2)}) %all-to-all-start) | async-done | bytes 416 | tf_op jit(solution)/shard_map/all_to_all | solution.py:68
  23.8 3.5 %all-to-all-start.1 = ((bf16[4,48,1024]{2,1,0:T(8,128)(2,1)}), bf16[4,48,1024]{2,1,0:T(8,128)(2,1)S(1)}, u32[]{:S(2)}, u32[]{:S(2)}) async-start(bf16[4,48,1024]{2,1,0:T(8,128)(2,1)} %bitcast.4), calls=%async_computation.1 | async-start | bytes 786432 | tf_op jit(solution)/shard_map/all_to_all | solution.py:61
  27.4 10.5 %all-to-all-done.1 = bf16[4,48,1024]{2,1,0:T(8,128)(2,1)S(1)} async-done(((bf16[4,48,1024]{2,1,0:T(8,128)(2,1)}), bf16[4,48,1024]{2,1,0:T(8,128)(2,1)S(1)}, u32[]{:S(2)}, u32[]{:S(2)}) %all-to-all-start.1) | async-done | bytes 393248 | tf_op jit(solution)/shard_map/all_to_all | solution.py:61
  38.0 1.4 %fusion.17 = bf16[192,768]{1,0:T(8,128)(2,1)} fusion(bf16[192,1024]{1,0:T(8,128)(2,1)S(1)} %bitcast.57, bf16[1,1,768,1024]{3,2,1,0:T(8,128)(2,1)S(1)} %copy-done), kind=kOutput, calls=%fused_computation.12 | convolution fusion | flops 302137344 | bytes 2260992 | tf_op jit(solution)/shard_map/dot_general | solution.py:80
  39.4 16.7 %all-gather.3.cloned.1.call-done = bf16[768,768]{1,0:T(8,128)(2,1)} async-done(((bf16[192,768]{1,0:T(8,128)(2,1)}), bf16[768,768]{1,0:T(8,128)(2,1)}) %all-gather.3.cloned.1.call-update) | async-done | bytes 1179664 | tf_op jit(solution)/shard_map/all_gather | solution.py:8
  56.1 1.5 %reduce_sum.57 = bf16[192,768]{1,0:T(8,128)(2,1)S(1)} reduce(bf16[4,192,768]{2,1,0:T(8,128)(2,1)} %bitcast.62, bf16[]{:T(256)} %constant.12.clone.1), dimensions={0}, to_apply=%region_4.5 | reduce | flops 442368 | bytes 1474562 | tf_op jit(solution)/shard_map/reduce_sum | solution.py:9
  57.6 1.2 %fusion.23 = (bf16[1,1,4,48,768]{4,3,2,1,0:T(8,128)(2,1)S(1)}, bf16[1,1,4,48,768]{4,3,2,1,0:T(8,128)(2,1)}, bf16[1,1,4,48,768]{4,3,2,1,0:T(8,128)(2,1)}) fusion(bf16[1,1,4,48,768]{4,3,2,1,0:T(8,128)(2,1)S(1)} %copy-done.4, bf16[1,1,4,48,768]{4,3,2,1,0:T(8,128)(2,1)S(1)} %copy-done.5, bf16[1,1,4,48,768]{4,3,2,1,0:T(8,128)(2,1)S(1)} %bitcast.61), kind=kLoop, calls=%fused_computation.26 | loop fusion | flops 2654208 | bytes 1769472 | tf_op jit(solution)/shard_map/convert_element_type | solution.py:84
  58.8 1.2 %fusion.14 = bf16[192,1024]{1,0:T(8,128)(2,1)} fusion(bf16[192,768]{1,0:T(8,128)(2,1)S(1)} %bitcast.59, bf16[1,1,768,1024]{3,2,1,0:T(8,128)(2,1)S(1)} %copy-done), kind=kOutput, calls=%fused_computation.10 | convolution fusion | flops 302186496 | bytes 2260992 | tf_op jit(solution)/shard_map/dot_general | solution.py:85
  60.1 4.7 %all-to-all-start.3 = ((bf16[4,48,1024]{2,1,0:T(8,128)(2,1)}), bf16[4,48,1024]{2,1,0:T(8,128)(2,1)S(1)}, u32[]{:S(2)}, u32[]{:S(2)}) async-start(bf16[4,48,1024]{2,1,0:T(8,128)(2,1)} %bitcast.56), calls=%async_computation.3 | async-start | bytes 786432 | tf_op jit(solution)/shard_map/all_to_all | solution.py:104
  64.8 2.2 %fusion = f32[192,1024]{1,0:T(8,128)S(1)} fusion(bf16[192,768]{1,0:T(8,128)(2,1)} %bitcast.60, bf16[1,1,1024,768]{3,2,1,0:T(8,128)(2,1)} %param.12), kind=kOutput, calls=%fused_computation | convolution fusion | flops 301989888 | bytes 2654208 | tf_op jit(solution)/shard_map/dot_general | solution.py:94
  67.0 1.4 %fusion.11 = bf16[192,1024]{1,0:T(8,128)(2,1)} fusion(f32[192,1024]{1,0:T(8,128)S(1)} %fusion, bf16[192,768]{1,0:T(8,128)(2,1)S(1)} %bitcast.58, bf16[1,1,1024,768]{3,2,1,0:T(8,128)(2,1)S(1)} %copy-done.1), kind=kOutput, calls=%fused_computation.9 | convolution fusion | flops 302383104 | bytes 3047424 | tf_op jit(solution)/shard_map/dot_general | solution.py:93
  68.4 8.4 %all-to-all-done.3 = bf16[4,48,1024]{2,1,0:T(8,128)(2,1)S(1)} async-done(((bf16[4,48,1024]{2,1,0:T(8,128)(2,1)}), bf16[4,48,1024]{2,1,0:T(8,128)(2,1)S(1)}, u32[]{:S(2)}, u32[]{:S(2)}) %all-to-all-start.3) | async-done | bytes 393248 | tf_op jit(solution)/shard_map/all_to_all | solution.py:104
  76.9 3.5 %all-to-all-start.2 = ((bf16[4,48,1024]{2,1,0:T(8,128)(2,1)}), bf16[4,48,1024]{2,1,0:T(8,128)(2,1)S(1)}, u32[]{:S(2)}, u32[]{:S(2)}) async-start(bf16[4,48,1024]{2,1,0:T(8,128)(2,1)} %bitcast.14), calls=%async_computation.2 | async-start | bytes 786432 | tf_op jit(solution)/shard_map/all_to_all | solution.py:97
  80.3 1.2 %fusion.22 = bf16[192]{0:T(256)(128)(2,1)S(1)} fusion(bf16[192,1024]{1,0:T(8,128)(2,1)S(1)} %bitcast.54, bf16[192,1024]{1,0:T(8,128)(2,1)} %convolution_convert_fusion), kind=kLoop, calls=%fused_computation.21 | loop fusion | flops 786240 | bytes 786816 | tf_op jit(solution)/shard_map/reduce_sum | solution.py:106
  81.5 6.0 %psum.7 = bf16[192]{0:T(256)(128)(2,1)S(1)} all-reduce(bf16[192]{0:T(256)(128)(2,1)S(1)} %fusion.22), channel_id=1, replica_groups=mesh['section'=2,'dp'=4,'expert'=4] {'dp'}, use_global_device_ids=true, to_apply=%region_6.7 | all-reduce | flops 192 | bytes 768 | tf_op jit(solution)/shard_map/psum | solution.py:111
  87.5 4.0 %all-to-all-done.2 = bf16[4,48,1024]{2,1,0:T(8,128)(2,1)S(1)} async-done(((bf16[4,48,1024]{2,1,0:T(8,128)(2,1)}), bf16[4,48,1024]{2,1,0:T(8,128)(2,1)S(1)}, u32[]{:S(2)}, u32[]{:S(2)}) %all-to-all-start.2) | async-done | bytes 393248 | tf_op jit(solution)/shard_map/all_to_all | solution.py:97
  91.7 1.3 %collective-permute-start = (bf16[64,1024]{1,0:T(8,128)(2,1)S(1)}, bf16[64,1024]{1,0:T(8,128)(2,1)S(1)}, u32[]{:S(2)}, u32[]{:S(2)}) collective-permute-start(bf16[64,1024]{1,0:T(8,128)(2,1)S(1)} %fusion.20), channel_id=1, source_target_pairs={{16,0},{17,1},{18,2},{19,3},{20,4},{21,5},{22,6},{23,7},{24,8},{25... | collective-permute-start | bytes 393224 | tf_op jit(solution)/shard_map/ppermute | solution.py:16
  94.0 4.6 %collective-permute-done = bf16[64,1024]{1,0:T(8,128)(2,1)S(1)} collective-permute-done((bf16[64,1024]{1,0:T(8,128)(2,1)S(1)}, bf16[64,1024]{1,0:T(8,128)(2,1)S(1)}, u32[]{:S(2)}, u32[]{:S(2)}) %collective-permute-start) | collective-permute-done | bytes 131104 | tf_op jit(solution)/shard_map/ppermute | solution.py:16
  (41 shorter events, 5.1 us)
Async XLA Ops:
  7.2 30.8 %copy-start = (bf16[1,1,768,1024]{3,2,1,0:T(8,128)(2,1)S(1)}, bf16[1,1,768,1024]{3,2,1,0:T(8,128)(2,1)}, u32[]{:S(2)}) copy-start(bf16[1,1,768,1024]{3,2,1,0:T(8,128)(2,1)} %param.13) | copy-start | bytes 4718596
  11.9 11.9 %all-to-all-start = ((bf16[4,1,48]{2,1,0:T(2,128)(2,1)}), bf16[4,1,48]{2,1,0:T(2,128)(2,1)S(1)}, u32[]{:S(2)}, u32[]{:S(2)}) async-start(bf16[4,1,48]{2,1,0:T(2,128)(2,1)} %all_to_all.20), calls=%async_computation | async-start | bytes 4096 | tf_op jit(solution)/shard_map/all_to_all | solution.py:68
  19.0 0.6 copy-start.6
  23.8 14.0 %all-to-all-start.1 = ((bf16[4,48,1024]{2,1,0:T(8,128)(2,1)}), bf16[4,48,1024]{2,1,0:T(8,128)(2,1)S(1)}, u32[]{:S(2)}, u32[]{:S(2)}) async-start(bf16[4,48,1024]{2,1,0:T(8,128)(2,1)} %bitcast.4), calls=%async_computation.1 | async-start | bytes 786432 | tf_op jit(solution)/shard_map/all_to_all | solution.py:61
  27.3 28.8 %all-gather.3.cloned.1.call-start = ((), (), s32[]{:S(2)}) async-start(), calls=%async_computation.4 | async-start | bytes 1474560 | tf_op jit(solution)/shard_map/all_gather | solution.py:8
  38.0 19.7 %copy-start.4 = (bf16[1,1,4,48,768]{4,3,2,1,0:T(8,128)(2,1)S(1)}, bf16[1,1,4,48,768]{4,3,2,1,0:T(8,128)(2,1)}, u32[]{:S(2)}) copy-start(bf16[1,1,4,48,768]{4,3,2,1,0:T(8,128)(2,1)} %param.15) | copy-start | bytes 884740
  38.0 19.6 %copy-start.5 = (bf16[1,1,4,48,768]{4,3,2,1,0:T(8,128)(2,1)S(1)}, bf16[1,1,4,48,768]{4,3,2,1,0:T(8,128)(2,1)}, u32[]{:S(2)}) copy-start(bf16[1,1,4,48,768]{4,3,2,1,0:T(8,128)(2,1)} %param.14) | copy-start | bytes 884740
  60.1 6.9 %copy-start.1 = (bf16[1,1,1024,768]{3,2,1,0:T(8,128)(2,1)S(1)}, bf16[1,1,1024,768]{3,2,1,0:T(8,128)(2,1)}, u32[]{:S(2)}) copy-start(bf16[1,1,1024,768]{3,2,1,0:T(8,128)(2,1)} %param.11) | copy-start | bytes 4718596
  60.1 16.8 %all-to-all-start.3 = ((bf16[4,48,1024]{2,1,0:T(8,128)(2,1)}), bf16[4,48,1024]{2,1,0:T(8,128)(2,1)S(1)}, u32[]{:S(2)}, u32[]{:S(2)}) async-start(bf16[4,48,1024]{2,1,0:T(8,128)(2,1)} %bitcast.56), calls=%async_computation.3 | async-start | bytes 786432 | tf_op jit(solution)/shard_map/all_to_all | solution.py:104
  64.8 2.2 %copy-start.2 = (bf16[1,1,4,48,768]{4,3,2,1,0:T(8,128)(2,1)S(1)}, bf16[1,1,4,48,768]{4,3,2,1,0:T(8,128)(2,1)}, u32[]{:S(2)}) copy-start(bf16[1,1,4,48,768]{4,3,2,1,0:T(8,128)(2,1)} %get-tuple-element.13) | copy-start | bytes 884740
  68.4 23.1 %copy-start.3 = (bf16[1,64,1024]{2,1,0:T(8,128)(2,1)S(1)}, bf16[1,64,1024]{2,1,0:T(8,128)(2,1)}, u32[]{:S(2)}) copy-start(bf16[1,64,1024]{2,1,0:T(8,128)(2,1)} %param.8) | copy-start | bytes 393220
  68.4 23.1 %copy-start.7 = (bf16[192,64]{0,1:T(8,128)(2,1)S(1)}, bf16[192,64]{0,1:T(8,128)(2,1)}, u32[]{:S(2)}) copy-start(bf16[192,64]{0,1:T(8,128)(2,1)} %copy-done.6) | copy-start | bytes 73732
  76.9 14.7 %all-to-all-start.2 = ((bf16[4,48,1024]{2,1,0:T(8,128)(2,1)}), bf16[4,48,1024]{2,1,0:T(8,128)(2,1)S(1)}, u32[]{:S(2)}, u32[]{:S(2)}) async-start(bf16[4,48,1024]{2,1,0:T(8,128)(2,1)} %bitcast.14), calls=%async_computation.2 | async-start | bytes 786432 | tf_op jit(solution)/shard_map/all_to_all | solution.py:97
  91.7 6.9 %collective-permute-start = (bf16[64,1024]{1,0:T(8,128)(2,1)S(1)}, bf16[64,1024]{1,0:T(8,128)(2,1)S(1)}, u32[]{:S(2)}, u32[]{:S(2)}) collective-permute-start(bf16[64,1024]{1,0:T(8,128)(2,1)S(1)} %fusion.20), channel_id=1, source_target_pairs={{16,0},{17,1},{18,2},{19,3},{20,4},{21,5},{22,6},{23,7},{24,8},{25... | collective-permute-start | bytes 393224 | tf_op jit(solution)/shard_map/ppermute | solution.py:16
Sparse Core Ops, SparseCore 0:
  39.5 16.5 all-gather.2
